TPU v7x, 512 devices: a whole 4x4x16 slice. The times are simulated.
512 devices in a mesh: pool: 32 (over y, z_lo, core), col: 16 (over x, z_hi).
Axes of the slice: x: 4, y: 4, z: 16 (z_hi: 4, z_lo: 4; z = z_hi * 4 + z_lo), core: 2. Of those that a mesh axis runs over, the one named last changes fastest.
Arguments:
- matrix_elems: bfloat16 [512, 64, 32768], P(None, 'pool', 'col'), may hold values from -6 to 6
- residue: bfloat16 [1024, 32768], P('pool', 'col'), may hold values from -6 to 6
- pole_freq: bfloat16 [1024, 32768], P('pool', 'col'), may hold values from 0.5 to 4
- slab_index: int32 [1024], P('col'), may hold values from 0 to 32767, as said below
- band_order: int32 [64], replicated, may hold values from 0 to 63, each once
- band_mag: float32 [64], replicated, may hold values from 0.1 to 8
Outputs:
- self_energy: float32 [512, 512], P('col')
Inputs may be any that keep to these rules, and one draw needn't show every extreme that they name: Block i of slab_index (positions i * 64 to (i + 1) * 64 - 1) holds distinct increasing G-vectors of i * 2048 to (i + 1) * 2048 - 1.
All inputs are finite; a program needn't handle non-finite values.
Results may differ from a plain program's by a relative error of at most 0.004.
Values may be sent and summed in bfloat16 or wider, within the bound.
A program may use at most 128 MiB of HBM per device.

v0:
```python
import jax
import jax.numpy as jnp
from jax import lax
from jax.sharding import PartitionSpec as P

broadening = 0.25


def pole_weights(res_rows, pole_rows, magnitude, parity):
    detuning = pole_rows.astype(jnp.float32)[None] + magnitude[:, None, None]
    signed_gap = parity[:, None, None] * detuning
    scaled = (
        res_rows.astype(jnp.float32)[None]
        * signed_gap
        / (signed_gap * signed_gap + broadening * broadening)
    )
    return scaled.astype(jnp.bfloat16)


def on_device(matrix_elems, residue, pole_freq, slab_index, band_order, band_mag):
    pool_count = lax.axis_size("pool")
    col_count = lax.axis_size("col")
    pool_at = lax.axis_index("pool")
    col_at = lax.axis_index("col")
    band_total = band_order.shape[0]
    occupied = band_total // 4
    states = matrix_elems.shape[0]
    members = matrix_elems.shape[1]
    column_count = matrix_elems.shape[2]
    slab_total = residue.shape[0] * pool_count
    ordinals = lax.dynamic_slice_in_dim(band_order, pool_at * members, members)
    matches = ordinals[:, None] == jnp.arange(band_total, dtype=jnp.int32)[None, :]
    magnitude = jnp.sum(jnp.where(matches, band_mag[None, :], 0.0), axis=1)
    parity = jnp.where(ordinals < occupied, 1.0, -1.0).astype(jnp.float32)
    local_rows = slab_index - col_at * column_count
    picked = jnp.take(matrix_elems, local_rows, axis=2)
    slab_elems = lax.all_gather(picked, "col", axis=2, tiled=True)
    gathered_poles = lax.all_gather(pole_freq, "pool", axis=0, tiled=True)
    weights = pole_weights(
        lax.all_gather(residue, "pool", axis=0, tiled=True), gathered_poles, magnitude, parity
    )
    mixed_rows = jnp.einsum(
        "njr,jrg->jng", slab_elems, weights, preferred_element_type=jnp.float32
    ).astype(jnp.bfloat16)
    normalizer = 1.0 / jnp.sqrt(jnp.float32(band_total) * slab_total * column_count * col_count)
    running = jnp.zeros((states // col_count * lax.axis_size("col"), states), jnp.float32)
    for member in range(members):
        left_part = mixed_rows[member]
        running = running + lax.dot_general(
            left_part,
            matrix_elems[:, member, :],
            (((1,), (1,)), ((), ())),
            preferred_element_type=jnp.float32,
        )
    owned_rows = lax.psum_scatter(running * normalizer, "col", scatter_dimension=0, tiled=True)
    self_energy = lax.psum(owned_rows, "pool")
    return self_energy


def solution(mesh):
    placed = (P(None, "pool", "col"), P("pool", "col"), P("pool", "col"), P("col"), P(), P())
    return jax.shard_map(
        on_device, mesh=mesh, in_specs=placed, out_specs=P("col", None), check_vma=False
    )
```

profile of v0, /device:TPU:2, one launch (start us, length us, event | category | flops | bytes accessed | tf_op | source)
XLA Modules:
  0.0 633.1 jit_solution(1917082151361824840)
XLA Ops:
  6.5 0.0 all-gather.8.cloned.1.call-start
  6.5 0.7 all-gather.8.cloned.1.call-update
  7.3 0.0 all-gather.6.cloned.1.call-start
  7.3 0.7 all-gather.6.cloned.1.call-update
  8.0 0.0 all-gather.4.cloned.1.call-start
  8.1 0.0 copy-start.2
  8.1 0.0 copy-start.3
  8.1 0.0 copy-start.4
  8.1 16.0 %copy.11 = bf16[512,2,2048]{0,1,2:T(2,128)(2,1)} copy(bf16[512,2,2048]{2,1,0:T(2,128)(2,1)} %param.6) | data formatting | bytes 8388608 | tf_op args[0]
  24.1 0.0 copy-done.2
  24.1 3.0 gather_fusion
  27.2 0.7 fusion.11
  27.9 0.0 all-gather.4.cloned.1.call-update
  27.9 0.0 reduce-scatter.2.cloned.1.call-start
  28.0 0.0 copy-done.3
  28.0 0.1 compare_select_fusion.2
  28.1 0.0 copy-done.4
  28.1 0.2 fusion.12
  28.3 10.4 %fusion.14 = (bf16[512,1,2048]{2,1,0:T(2,128)(2,1)}, bf16[512,1,2048]{2,1,0:T(2,128)(2,1)}) fusion(bf16[512,2,2048]{2,1,0:T(2,128)(2,1)} %param.6), kind=kLoop, calls=%fused_computation.26 | loop fusion | bytes 8388608 | tf_op jit(solution)/shard_map/slice | solution.py:51
  38.6 43.4 %all-gather.8.cloned.1.call-done = bf16[1024,2048]{1,0:T(8,128)(2,1)} async-done(((bf16[32,2048]{1,0:T(8,128)(2,1)}), bf16[1024,2048]{1,0:T(8,128)(2,1)}) %all-gather.8.cloned.1.call-update) | async-done | bytes 4194320 | tf_op jit(solution)/shard_map/all_gather | solution.py:38
  82.0 6.5 %convert_element_type.13 = f32[1024,2048]{1,0:T(8,128)} convert(bf16[1024,2048]{1,0:T(8,128)(2,1)} %all-gather.8.cloned.1.call-done) | non-fusion elementwise | flops 2097152 | bytes 12582912 | tf_op jit(solution)/shard_map/convert_element_type | solution.py:10
  88.5 62.7 %all-gather.6.cloned.1.call-done = bf16[1024,2048]{1,0:T(8,128)(2,1)} async-done(((bf16[32,2048]{1,0:T(8,128)(2,1)}), bf16[1024,2048]{1,0:T(8,128)(2,1)}) %all-gather.6.cloned.1.call-update) | async-done | bytes 4194320 | tf_op jit(solution)/shard_map/all_gather | solution.py:40
  151.2 6.5 %convert_element_type.12 = f32[1024,2048]{1,0:T(8,128)} convert(bf16[1024,2048]{1,0:T(8,128)(2,1)} %all-gather.6.cloned.1.call-done) | non-fusion elementwise | flops 2097152 | bytes 12582912 | tf_op jit(solution)/shard_map/convert_element_type | solution.py:13
  157.7 89.2 %all-gather.4.cloned.1.call-done = bf16[512,2,1024]{0,2,1:T(8,128)(2,1)} async-done(((bf16[512,2,64]{0,2,1:T(8,128)(2,1)}), bf16[512,2,1024]{0,2,1:T(8,128)(2,1)}) %all-gather.4.cloned.1.call-update) | async-done | bytes 2097168 | tf_op jit(solution)/shard_map/all_gather | solution.py:37
  246.9 0.0 copy-start.1
  246.9 11.3 %fusion.6 = bf16[2,512,2048]{2,1,0:T(8,128)(2,1)S(1)} fusion(bf16[512,2,1024]{0,2,1:T(8,128)(2,1)} %all-gather.4.cloned.1.call-done, f32[2]{0:T(128)S(1)} %fusion.12, f32[1024,2048]{1,0:T(8,128)} %convert_element_type.13, f32[2]{0:T(128)S(1)} %get-tuple-element.5, f32[1024,2048]{1,0:T(8,128)} %convert_element_type.12), kind=kOutput, calls=%fused_computation.8 | convolution fusion | flops 4326424576 | bytes 23068688 | tf_op jit(solution)/shard_map/njr,jrg->jng/dot_general | solution.py:42
  258.2 0.0 copy-done.1
  258.2 0.0 copy-start
  258.2 1.7 fusion.7
  259.9 0.5 copy-done
  260.4 2.6 fusion.10
  263.0 0.0 reduce-scatter.2.cloned.1.call-update
  263.0 0.0 all-reduce.2.cloned.1.call-start
  263.1 109.1 %reduce-scatter.2.cloned.1.call-done = f32[32,512]{1,0:T(8,128)} async-done(((f32[512,512]{1,0:T(8,128)}), f32[32,512]{1,0:T(8,128)}) %reduce-scatter.2.cloned.1.call-update) | async-done | bytes 65552 | tf_op jit(solution)/shard_map/reduce_scatter | solution.py:55
  372.2 0.0 all-reduce.2.cloned.1.call-update
  372.2 252.9 %all-reduce.2.cloned.1.call-done = f32[32,512]{1,0:T(8,128)} async-done(((f32[32,512]{1,0:T(8,128)}), f32[32,512]{1,0:T(8,128)}) %all-reduce.2.cloned.1.call-update) | async-done | bytes 65552 | tf_op jit(solution)/shard_map/psum | solution.py:56
  625.1 1.5 copy.29
  (2 shorter events, 0.0 us)
Async XLA Ops:
  6.5 75.5 %all-gather.8.cloned.1.call-start = ((), (), s32[]{:S(2)}) async-start(), calls=%async_computation.3 | async-start | bytes 4325376 | tf_op jit(solution)/shard_map/all_gather | solution.py:38
  7.3 143.9 %all-gather.6.cloned.1.call-start = ((), (), s32[]{:S(2)}) async-start(), calls=%async_computation.2 | async-start | bytes 4325376 | tf_op jit(solution)/shard_map/all_gather | solution.py:40
  8.0 238.8 %all-gather.4.cloned.1.call-start = ((), (), s32[]{:S(2)}) async-start(), calls=%async_computation.1 | async-start | bytes 2228224 | tf_op jit(solution)/shard_map/all_gather | solution.py:37
  8.1 16.1 %copy-start.2 = (s32[64]{0:T(128)S(1)}, s32[64]{0:T(128)}, u32[]{:S(2)}) copy-start(s32[64]{0:T(128)} %param.9) | copy-start | bytes 772
  8.1 19.9 %copy-start.3 = (s32[64]{0:T(128)S(1)}, s32[64]{0:T(128)}, u32[]{:S(2)}) copy-start(s32[64]{0:T(128)} %param.10) | copy-start | bytes 772
  8.1 20.0 %copy-start.4 = (f32[64]{0:T(128)S(1)}, f32[64]{0:T(128)}, u32[]{:S(2)}) copy-start(f32[64]{0:T(128)} %param.11) | copy-start | bytes 772
  27.9 344.2 %reduce-scatter.2.cloned.1.call-start = ((), (), s32[]{:S(2)}) async-start(), calls=%async_computation.4 | async-start | bytes 1114112 | tf_op jit(solution)/shard_map/reduce_scatter | solution.py:55
  246.9 11.4 %copy-start.1 = (bf16[512,1,2048]{2,1,0:T(2,128)(2,1)S(1)}, bf16[512,1,2048]{2,1,0:T(2,128)(2,1)}, u32[]{:S(2)}) copy-start(bf16[512,1,2048]{2,1,0:T(2,128)(2,1)} %get-tuple-element.10) | copy-start | bytes 6291460
  258.2 2.2 copy-start
  263.0 362.1 %all-reduce.2.cloned.1.call-start = ((), (), s32[]{:S(2)}) async-start(), calls=%async_computation.5 | async-start | bytes 131072 | tf_op jit(solution)/shard_map/psum | solution.py:56
Sparse Core Ops, SparseCore 0:
  9.5 72.4 all-gather.7
  84.2 66.9 all-gather.5
  154.3 92.5 all-gather.3
  263.2 108.9 reduce-scatter.1
  375.2 249.8 all-reduce.1
where the time goes:
time: 634 us; the launch traced here: 633 us
  waiting for transfers between devices  559 us (88%)
  local copies, waits for them, and re-layouts  31.4 us (5%)
  matrix products  15.6 us (2%)
  other arithmetic  14 us (2%)
  between operations  13.2 us (2%)
    psum x1, waiting for transfers between devices, on_device(): self_energy = lax.psum(owned_rows, 'pool')  253 us
    reduce_scatter x1, waiting for transfers between devices, on_device(): lax.psum_scatter(running * normalizer, 'col', scatter_dimension=0, tiled=...  109 us
    all_gather x1, waiting for transfers between devices, on_device(): slab_elems = lax.all_gather(picked, 'col', axis=2, tiled=True)  89.2 us
    all_gather x1, waiting for transfers between devices, on_device(): lax.all_gather(residue, 'pool', axis=0, tiled=True)  62.7 us
    all_gather x1, waiting for transfers between devices, on_device(): gathered_poles = lax.all_gather(pole_freq, 'pool', axis=0, tiled=True)  43.4 us
    unnamed x12, local copies, waits for them, and re-layouts  18 us
  transfers between devices with their start and end apart: 5, of which 5 were waited for; matrix products, arithmetic and copies ran while one was open for 7% of the time, Pallas kernels for 0%

commit v1 on v0

--- a/solution.py
+++ b/solution.py
@@ -4,6 +4,12 @@
 from jax.sharding import PartitionSpec as P
 
 broadening = 0.25
+
+
+def gather_and_add(x, name):
+    parts = lax.all_gather(x, name, axis=0, tiled=False)
+    acc = parts.sum(axis=0)
+    return acc
 
 
 def pole_weights(res_rows, pole_rows, magnitude, parity):
@@ -53,7 +59,7 @@
             preferred_element_type=jnp.float32,
         )
     owned_rows = lax.psum_scatter(running * normalizer, "col", scatter_dimension=0, tiled=True)
-    self_energy = lax.psum(owned_rows, "pool")
+    self_energy = gather_and_add(owned_rows, "pool")
     return self_energy
 
 

time: 634 us -> 446 us (0.70)
  the two profiles are of different devices: /device:TPU:2 before, /device:TPU:1 now
where the time goes in v1:
time: 446 us; the launch traced here: 445 us
  waiting for transfers between devices  370 us (83%)
  local copies, waits for them, and re-layouts  29.9 us (7%)
  other arithmetic  16.3 us (4%)
  matrix products  15.6 us (3%)
  between operations  13.2 us (3%)
    reduce_scatter x1, waiting for transfers between devices, on_device(): lax.psum_scatter(running * normalizer, 'col', scatter_dimension=0, tiled=...  109 us
    all_gather x1, waiting for transfers between devices, on_device(): slab_elems = lax.all_gather(picked, 'col', axis=2, tiled=True)  89.5 us
    all_gather x1, waiting for transfers between devices, gather_and_add(): parts = lax.all_gather(x, name, axis=0, tiled=False)  63.1 us
    all_gather x1, waiting for transfers between devices, on_device(): lax.all_gather(residue, 'pool', axis=0, tiled=True)  62.7 us
    all_gather x1, waiting for transfers between devices, on_device(): gathered_poles = lax.all_gather(pole_freq, 'pool', axis=0, tiled=True)  44.7 us
    unnamed x11, local copies, waits for them, and re-layouts  16.5 us
    dot_general x1, matrix products, on_device(): jnp.einsum('njr,jrg->jng', slab_elems, weights, preferred_element_type=jn...  11.3 us
    slice x1, local copies, waits for them, and re-layouts, on_device(): matrix_elems[:, member, :]  10.4 us
  transfers between devices with their start and end apart: 5, of which 5 were waited for; matrix products, arithmetic and copies ran while one was open for 10% of the time, Pallas kernels for 0%

profile of v1, /device:TPU:1, one launch (start us, length us, event | category | flops | bytes accessed | tf_op | source)
XLA Modules:
  0.0 445.3 jit_solution(2480759705708391809)
XLA Ops:
  6.5 0.0 all-gather.10.cloned.1.call-start
  6.5 0.7 all-gather.10.cloned.1.call-update
  7.3 0.0 all-gather.8.cloned.1.call-start
  7.3 0.7 all-gather.8.cloned.1.call-update
  8.0 0.0 all-gather.6.cloned.1.call-start
  8.1 0.0 copy-start.2
  8.1 0.0 copy-start.3
  8.1 0.0 copy-start.4
  8.1 16.0 %copy.11 = bf16[512,2,2048]{0,1,2:T(2,128)(2,1)} copy(bf16[512,2,2048]{2,1,0:T(2,128)(2,1)} %param.6) | data formatting | bytes 8388608 | tf_op args[0]
  24.1 0.0 copy-done.2
  24.1 3.0 gather_fusion
  27.2 0.7 fusion.11
  27.9 0.0 all-gather.6.cloned.1.call-update
  27.9 0.0 reduce-scatter.2.cloned.1.call-start
  28.0 0.0 copy-done.3
  28.0 0.1 compare_select_fusion.2
  28.1 0.0 copy-done.4
  28.1 0.2 fusion.12
  28.3 10.4 %fusion.14 = (bf16[512,1,2048]{2,1,0:T(2,128)(2,1)}, bf16[512,1,2048]{2,1,0:T(2,128)(2,1)}) fusion(bf16[512,2,2048]{2,1,0:T(2,128)(2,1)} %param.6), kind=kLoop, calls=%fused_computation.26 | loop fusion | bytes 8388608 | tf_op jit(solution)/shard_map/slice | solution.py:57
  38.6 44.7 %all-gather.10.cloned.1.call-done = bf16[1024,2048]{1,0:T(8,128)(2,1)} async-done(((bf16[32,2048]{1,0:T(8,128)(2,1)}), bf16[1024,2048]{1,0:T(8,128)(2,1)}) %all-gather.10.cloned.1.call-update) | async-done | bytes 4194320 | tf_op jit(solution)/shard_map/all_gather | solution.py:44
  83.3 6.5 %convert_element_type.13 = f32[1024,2048]{1,0:T(8,128)} convert(bf16[1024,2048]{1,0:T(8,128)(2,1)} %all-gather.10.cloned.1.call-done) | non-fusion elementwise | flops 2097152 | bytes 12582912 | tf_op jit(solution)/shard_map/convert_element_type | solution.py:16
  89.8 62.7 %all-gather.8.cloned.1.call-done = bf16[1024,2048]{1,0:T(8,128)(2,1)} async-done(((bf16[32,2048]{1,0:T(8,128)(2,1)}), bf16[1024,2048]{1,0:T(8,128)(2,1)}) %all-gather.8.cloned.1.call-update) | async-done | bytes 4194320 | tf_op jit(solution)/shard_map/all_gather | solution.py:46
  152.5 6.5 %convert_element_type.12 = f32[1024,2048]{1,0:T(8,128)} convert(bf16[1024,2048]{1,0:T(8,128)(2,1)} %all-gather.8.cloned.1.call-done) | non-fusion elementwise | flops 2097152 | bytes 12582912 | tf_op jit(solution)/shard_map/convert_element_type | solution.py:19
  159.0 89.5 %all-gather.6.cloned.1.call-done = bf16[512,2,1024]{0,2,1:T(8,128)(2,1)} async-done(((bf16[512,2,64]{0,2,1:T(8,128)(2,1)}), bf16[512,2,1024]{0,2,1:T(8,128)(2,1)}) %all-gather.6.cloned.1.call-update) | async-done | bytes 2097168 | tf_op jit(solution)/shard_map/all_gather | solution.py:43
  248.5 0.0 copy-start.1
  248.5 11.3 %fusion.6 = bf16[2,512,2048]{2,1,0:T(8,128)(2,1)S(1)} fusion(bf16[512,2,1024]{0,2,1:T(8,128)(2,1)} %all-gather.6.cloned.1.call-done, f32[2]{0:T(128)S(1)} %fusion.12, f32[1024,2048]{1,0:T(8,128)} %convert_element_type.13, f32[2]{0:T(128)S(1)} %get-tuple-element.5, f32[1024,2048]{1,0:T(8,128)} %convert_element_type.12), kind=kOutput, calls=%fused_computation.8 | convolution fusion | flops 4326424576 | bytes 23068688 | tf_op jit(solution)/shard_map/njr,jrg->jng/dot_general | solution.py:48
  259.8 0.0 copy-done.1
  259.9 0.0 copy-start
  259.9 1.7 fusion.7
  261.6 0.5 copy-done
  262.0 2.6 fusion.10
  264.7 0.0 reduce-scatter.2.cloned.1.call-update
  264.7 0.0 all-gather.12.cloned.1.call-start
  264.7 108.6 %reduce-scatter.2.cloned.1.call-done = f32[32,512]{1,0:T(8,128)} async-done(((f32[512,512]{1,0:T(8,128)}), f32[32,512]{1,0:T(8,128)}) %reduce-scatter.2.cloned.1.call-update) | async-done | bytes 65552 | tf_op jit(solution)/shard_map/reduce_scatter | solution.py:61
  373.3 0.0 all-gather.12.cloned.1.call-update
  373.3 63.1 %all-gather.12.cloned.1.call-done = f32[1024,512]{1,0:T(8,128)} async-done(((f32[32,512]{1,0:T(8,128)}), f32[1024,512]{1,0:T(8,128)}) %all-gather.12.cloned.1.call-update) | async-done | bytes 2097168 | tf_op jit(solution)/shard_map/all_gather | solution.py:10
  436.4 2.4 reduce_sum.19
  (2 shorter events, 0.0 us)
Async XLA Ops:
  6.5 76.8 %all-gather.10.cloned.1.call-start = ((), (), s32[]{:S(2)}) async-start(), calls=%async_computation.3 | async-start | bytes 4325376 | tf_op jit(solution)/shard_map/all_gather | solution.py:44
  7.3 145.2 %all-gather.8.cloned.1.call-start = ((), (), s32[]{:S(2)}) async-start(), calls=%async_computation.2 | async-start | bytes 4325376 | tf_op jit(solution)/shard_map/all_gather | solution.py:46
  8.0 240.5 %all-gather.6.cloned.1.call-start = ((), (), s32[]{:S(2)}) async-start(), calls=%async_computation.1 | async-start | bytes 2228224 | tf_op jit(solution)/shard_map/all_gather | solution.py:43
  8.1 16.1 %copy-start.2 = (s32[64]{0:T(128)S(1)}, s32[64]{0:T(128)}, u32[]{:S(2)}) copy-start(s32[64]{0:T(128)} %param.9) | copy-start | bytes 772
  8.1 19.9 %copy-start.3 = (s32[64]{0:T(128)S(1)}, s32[64]{0:T(128)}, u32[]{:S(2)}) copy-start(s32[64]{0:T(128)} %param.10) | copy-start | bytes 772
  8.1 20.0 %copy-start.4 = (f32[64]{0:T(128)S(1)}, f32[64]{0:T(128)}, u32[]{:S(2)}) copy-start(f32[64]{0:T(128)} %param.11) | copy-start | bytes 772
  27.9 345.4 %reduce-scatter.2.cloned.1.call-start = ((), (), s32[]{:S(2)}) async-start(), calls=%async_computation.4 | async-start | bytes 1114112 | tf_op jit(solution)/shard_map/reduce_scatter | solution.py:61
  248.5 11.3 %copy-start.1 = (bf16[512,1,2048]{2,1,0:T(2,128)(2,1)S(1)}, bf16[512,1,2048]{2,1,0:T(2,128)(2,1)}, u32[]{:S(2)}) copy-start(bf16[512,1,2048]{2,1,0:T(2,128)(2,1)} %get-tuple-element.10) | copy-start | bytes 6291460
  259.9 2.2 copy-start
  264.7 171.7 %all-gather.12.cloned.1.call-start = ((), (), s32[]{:S(2)}) async-start(), calls=%async_computation.5 | async-start | bytes 2162688 | tf_op jit(solution)/shard_map/all_gather | solution.py:10
Sparse Core Ops, SparseCore 0:
  9.5 73.7 all-gather.9
  85.4 66.9 all-gather.7
  155.5 92.9 all-gather.5
  264.8 108.4 reduce-scatter.1
  375.5 60.8 all-gather.11

commit v2 on v0

--- a/solution.py
+++ b/solution.py
@@ -2,6 +2,7 @@
 import jax.numpy as jnp
 from jax import lax
 from jax.sharding import PartitionSpec as P
+from jax.lax import all_to_all, axis_size
 
 broadening = 0.25
 
@@ -37,7 +38,18 @@
     slab_elems = lax.all_gather(picked, "col", axis=2, tiled=True)
     gathered_poles = lax.all_gather(pole_freq, "pool", axis=0, tiled=True)
     weights = pole_weights(
-        lax.all_gather(residue, "pool", axis=0, tiled=True), gathered_poles, magnitude, parity
+        jnp.concatenate(
+            all_to_all(
+                jnp.stack(axis_size("pool") * [residue], axis=0),
+                axis_name="pool",
+                split_axis=0,
+                concat_axis=0,
+            ),
+            axis=0,
+        ),
+        gathered_poles,
+        magnitude,
+        parity,
     )
     mixed_rows = jnp.einsum(
         "njr,jrg->jng", slab_elems, weights, preferred_element_type=jnp.float32

time: 634 us -> 612 us (0.965)
  waiting for transfers between devices: 559 us -> 524 us
  starting transfers between devices: 0.16 us -> 9.21 us
    all_gather x1 -> x0, waiting for transfers between devices: 62.7 us -> none  [on_device(): lax.all_gather(residue, 'pool', axis=0, tiled=True)]
    all_gather x1, waiting for transfers between devices: 43.4 us -> 76.7 us  [on_device(): gathered_poles = lax.all_gather(pole_freq, 'pool', axis=0, tiled=True)]
    all_to_all x0 -> x1, starting transfers between devices: none -> 9.05 us  [on_device(): all_to_all(jnp.stack(axis_size('pool') * [residue], axis=0), axis_name='p...]
  transfers between devices with their start and end apart: 5 -> 5, of which waited for: 5 -> 4; matrix products, arithmetic and copies ran while one was open for 7% -> 7% of each run, Pallas kernels for 0% -> 0%
where the time goes in v2:
time: 612 us; the launch traced here: 611 us
  waiting for transfers between devices  524 us (86%)
  local copies, waits for them, and re-layouts  34.8 us (6%)
  matrix products  15.6 us (3%)
  other arithmetic  14 us (2%)
  between operations  13.2 us (2%)
  starting transfers between devices  9.21 us (2%)
    psum x1, waiting for transfers between devices, on_device(): self_energy = lax.psum(owned_rows, 'pool')  253 us
    reduce_scatter x1, waiting for transfers between devices, on_device(): lax.psum_scatter(running * normalizer, 'col', scatter_dimension=0, tiled=...  109 us
    all_gather x1, waiting for transfers between devices, on_device(): slab_elems = lax.all_gather(picked, 'col', axis=2, tiled=True)  85.4 us
    all_gather x1, waiting for transfers between devices, on_device(): gathered_poles = lax.all_gather(pole_freq, 'pool', axis=0, tiled=True)  76.7 us
    unnamed x12, local copies, waits for them, and re-layouts  18 us
  transfers between devices with their start and end apart: 5, of which 4 were waited for; matrix products, arithmetic and copies ran while one was open for 7% of the time, Pallas kernels for 0%

profile of v2, /device:TPU:2, one launch (start us, length us, event | category | flops | bytes accessed | tf_op | source)
XLA Modules:
  0.0 611.2 jit_solution(7322605836376567961)
XLA Ops:
  6.5 3.4 stack.2
  9.9 9.0 %all-to-all-start = ((bf16[32,32,2048]{2,1,0:T(8,128)(2,1)}), bf16[32,32,2048]{2,1,0:T(8,128)(2,1)}, u32[]{:S(2)}, u32[]{:S(2)}) async-start(bf16[32,32,2048]{2,1,0:T(8,128)(2,1)} %stack.2), calls=%async_computation | async-start | bytes 8388608 | tf_op jit(solution)/shard_map/all_to_all | solution.py:42
  19.0 0.0 all-gather.5.cloned.1.call-start
  19.0 0.7 all-gather.5.cloned.1.call-update
  19.7 0.0 all-gather.3.cloned.1.call-start
  19.8 0.0 copy-start.2
  19.8 0.0 copy-start.3
  19.8 0.0 copy-start.4
  19.8 16.0 %copy.11 = bf16[512,2,2048]{0,1,2:T(2,128)(2,1)} copy(bf16[512,2,2048]{2,1,0:T(2,128)(2,1)} %param.6) | data formatting | bytes 8388608 | tf_op args[0]
  35.8 0.0 copy-done.2
  35.8 3.0 gather_fusion
  38.9 0.7 fusion.11
  39.6 0.0 all-gather.3.cloned.1.call-update
  39.6 0.0 reduce-scatter.2.cloned.1.call-start
  39.7 0.0 copy-done.3
  39.7 0.1 compare_select_fusion.2
  39.8 0.0 copy-done.4
  39.8 0.2 fusion.12
  39.9 10.4 %fusion.14 = (bf16[512,1,2048]{2,1,0:T(2,128)(2,1)}, bf16[512,1,2048]{2,1,0:T(2,128)(2,1)}) fusion(bf16[512,2,2048]{2,1,0:T(2,128)(2,1)} %param.6), kind=kLoop, calls=%fused_computation.27 | loop fusion | bytes 8388608 | tf_op jit(solution)/shard_map/slice | solution.py:63
  50.3 76.7 %all-gather.5.cloned.1.call-done = bf16[1024,2048]{1,0:T(8,128)(2,1)} async-done(((bf16[32,2048]{1,0:T(8,128)(2,1)}), bf16[1024,2048]{1,0:T(8,128)(2,1)}) %all-gather.5.cloned.1.call-update) | async-done | bytes 4194320 | tf_op jit(solution)/shard_map/all_gather | solution.py:39
  127.0 6.5 %convert_element_type.21 = f32[1024,2048]{1,0:T(8,128)} convert(bf16[1024,2048]{1,0:T(8,128)(2,1)} %all-gather.5.cloned.1.call-done) | non-fusion elementwise | flops 2097152 | bytes 12582912 | tf_op jit(solution)/shard_map/convert_element_type | solution.py:11
  133.5 0.0 all-to-all-done
  133.5 6.5 %bitcast_convert_fusion = f32[1024,2048]{1,0:T(8,128)} fusion(bf16[32,32,2048]{2,1,0:T(8,128)(2,1)} %all-to-all-done), kind=kLoop, calls=%fused_computation.8 | loop fusion | flops 2097152 | bytes 12582912 | tf_op jit(solution)/shard_map/convert_element_type | solution.py:14
  140.0 85.4 %all-gather.3.cloned.1.call-done = bf16[512,2,1024]{0,2,1:T(8,128)(2,1)} async-done(((bf16[512,2,64]{0,2,1:T(8,128)(2,1)}), bf16[512,2,1024]{0,2,1:T(8,128)(2,1)}) %all-gather.3.cloned.1.call-update) | async-done | bytes 2097168 | tf_op jit(solution)/shard_map/all_gather | solution.py:38
  225.4 0.0 copy-start.1
  225.4 11.3 %fusion.6 = bf16[2,512,2048]{2,1,0:T(8,128)(2,1)S(1)} fusion(bf16[512,2,1024]{0,2,1:T(8,128)(2,1)} %all-gather.3.cloned.1.call-done, f32[2]{0:T(128)S(1)} %fusion.12, f32[1024,2048]{1,0:T(8,128)} %convert_element_type.21, f32[2]{0:T(128)S(1)} %get-tuple-element.5, f32[1024,2048]{1,0:T(8,128)} %bitcast_convert_fusion), kind=kOutput, calls=%fused_computation.9 | convolution fusion | flops 4326424576 | bytes 23068688 | tf_op jit(solution)/shard_map/njr,jrg->jng/dot_general | solution.py:54
  236.7 0.0 copy-done.1
  236.8 0.0 copy-start
  236.8 1.7 fusion.7
  238.5 0.5 copy-done
  238.9 2.6 fusion.10
  241.6 0.0 reduce-scatter.2.cloned.1.call-update
  241.6 0.0 all-reduce.2.cloned.1.call-start
  241.6 109.0 %reduce-scatter.2.cloned.1.call-done = f32[32,512]{1,0:T(8,128)} async-done(((f32[512,512]{1,0:T(8,128)}), f32[32,512]{1,0:T(8,128)}) %reduce-scatter.2.cloned.1.call-update) | async-done | bytes 65552 | tf_op jit(solution)/shard_map/reduce_scatter | solution.py:67
  350.6 0.0 all-reduce.2.cloned.1.call-update
  350.7 252.5 %all-reduce.2.cloned.1.call-done = f32[32,512]{1,0:T(8,128)} async-done(((f32[32,512]{1,0:T(8,128)}), f32[32,512]{1,0:T(8,128)}) %all-reduce.2.cloned.1.call-update) | async-done | bytes 65552 | tf_op jit(solution)/shard_map/psum | solution.py:68
  603.2 1.5 copy.29
  (2 shorter events, 0.0 us)
Async XLA Ops:
  9.9 123.6 %all-to-all-start = ((bf16[32,32,2048]{2,1,0:T(8,128)(2,1)}), bf16[32,32,2048]{2,1,0:T(8,128)(2,1)}, u32[]{:S(2)}, u32[]{:S(2)}) async-start(bf16[32,32,2048]{2,1,0:T(8,128)(2,1)} %stack.2), calls=%async_computation | async-start | bytes 8388608 | tf_op jit(solution)/shard_map/all_to_all | solution.py:42
  19.0 108.0 %all-gather.5.cloned.1.call-start = ((), (), s32[]{:S(2)}) async-start(), calls=%async_computation.3 | async-start | bytes 4325376 | tf_op jit(solution)/shard_map/all_gather | solution.py:39
  19.7 205.7 %all-gather.3.cloned.1.call-start = ((), (), s32[]{:S(2)}) async-start(), calls=%async_computation.2 | async-start | bytes 2228224 | tf_op jit(solution)/shard_map/all_gather | solution.py:38
  19.8 16.0 %copy-start.2 = (s32[64]{0:T(128)S(1)}, s32[64]{0:T(128)}, u32[]{:S(2)}) copy-start(s32[64]{0:T(128)} %param.9) | copy-start | bytes 772
  19.8 19.9 %copy-start.3 = (s32[64]{0:T(128)S(1)}, s32[64]{0:T(128)}, u32[]{:S(2)}) copy-start(s32[64]{0:T(128)} %param.10) | copy-start | bytes 772
  19.8 20.0 %copy-start.4 = (f32[64]{0:T(128)S(1)}, f32[64]{0:T(128)}, u32[]{:S(2)}) copy-start(f32[64]{0:T(128)} %param.11) | copy-start | bytes 772
  39.6 311.0 %reduce-scatter.2.cloned.1.call-start = ((), (), s32[]{:S(2)}) async-start(), calls=%async_computation.4 | async-start | bytes 1114112 | tf_op jit(solution)/shard_map/reduce_scatter | solution.py:67
  225.4 11.4 %copy-start.1 = (bf16[512,1,2048]{2,1,0:T(2,128)(2,1)S(1)}, bf16[512,1,2048]{2,1,0:T(2,128)(2,1)}, u32[]{:S(2)}) copy-start(bf16[512,1,2048]{2,1,0:T(2,128)(2,1)} %get-tuple-element.10) | copy-start | bytes 6291460
  236.8 2.2 copy-start
  241.6 361.6 %all-reduce.2.cloned.1.call-start = ((), (), s32[]{:S(2)}) async-start(), calls=%async_computation.5 | async-start | bytes 131072 | tf_op jit(solution)/shard_map/psum | solution.py:68
Sparse Core Ops, SparseCore 0:
  22.0 104.9 all-gather.4
  130.1 95.2 all-gather.2
  241.7 108.8 reduce-scatter.1
  353.7 249.4 all-reduce.1
